TPU v7x, 256 devices: a whole 4x4x8 slice. The times are simulated.
256 devices in a mesh: row: 16 (over z_hi, x, core), col: 16 (over z_lo, y).
Axes of the slice: x: 4, y: 4, z: 8 (z_hi: 2, z_lo: 4; z = z_hi * 4 + z_lo), core: 2. Of those that a mesh axis runs over, the one named last changes fastest.
Arguments:
- features: bfloat16 [32768, 768], P(('row', 'col')), may hold values from -6 to 6
- self_weight: bfloat16 [768, 768], replicated, may hold values from -0.21875 to 0.21875
- rel_weight: bfloat16 [768, 5, 768], replicated, may hold values from -0.21875 to 0.21875
- bias: float32 [768], replicated, may hold values from -3 to 3
- blocks: bfloat16 [16, 16, 5, 8, 128, 128], P('row', 'col'), may hold values from -0.083496094 to 0.083496094
- block_rows: int32 [16, 16, 5, 8], P('row', 'col'), may hold values from 0 to 15
- block_cols: int32 [16, 16, 5, 8], P('row', 'col'), may hold values from 0 to 15
- block_counts: int32 [16, 16, 5], P('row', 'col'), may hold values from 1 to 8, as said below
Outputs:
- layer_out: bfloat16 [32768, 768], P(('row', 'col'))
Inputs may be any that keep to these rules, and one draw needn't show every extreme that they name: The live slots of a tile and relation are its first block_counts slots; the others are ignored. `block_rows`: pairs of destination and source blocks may repeat within a tile.
All inputs are finite; a program needn't handle non-finite values.
Results may differ from a plain program's by a relative error of at most 0.014.
Values may be sent and summed in bfloat16 or wider, within the bound.
No kernel may reach another device: no remote copies, remote signals or barrier semaphores. Data moves between devices by JAX's collectives and lax.ppermute only.
A program may use at most 128 MiB of HBM per device.

v0:
```python
import jax
import jax.numpy as jnp
from jax import lax
from jax.sharding import PartitionSpec as P


def aggregate_tile(tile_blocks, tile_rows, tile_cols, tile_counts, panel, brows):
    relations = tile_blocks.shape[0]
    slots = tile_blocks.shape[1]
    block_size = tile_blocks.shape[-1]
    width = panel.shape[-1]
    total = jnp.zeros((brows, block_size, width), jnp.float32)
    for relation in range(relations):
        source = panel[:, :, relation, :]
        chosen = source[tile_cols[relation]]
        live = lax.iota(jnp.int32, slots) < tile_counts[relation]
        owners = (
            (tile_rows[relation][None, :] == lax.iota(jnp.int32, brows)[:, None]) & live[None, :]
        ).astype(jnp.bfloat16)
        products = jnp.einsum(
            "sik,skd->sid", tile_blocks[relation], chosen, preferred_element_type=jnp.float32
        )
        upper = products.astype(jnp.bfloat16)
        lower = (products - upper.astype(jnp.float32)).astype(jnp.bfloat16)
        halves = jnp.stack([upper, lower], axis=1)
        routed = jnp.einsum("ns,shid->nid", owners, halves, preferred_element_type=jnp.float32)
        total = total + routed
    return total.reshape(brows * block_size, width)


def per_device(
    features, self_weight, rel_weight, bias, blocks, block_rows, block_cols, block_counts
):
    rows_dev, width = features.shape
    relations = rel_weight.shape[1]
    block_size = blocks.shape[-1]
    brows = rows_dev * lax.axis_size("col") // block_size
    bcols = rows_dev * lax.axis_size("row") // block_size
    stacked = rel_weight.reshape(width, relations * width)
    own_rows = jnp.dot(features, stacked, preferred_element_type=jnp.float32).astype(jnp.bfloat16)
    panel = lax.all_gather(own_rows, "row", axis=0, tiled=True)
    panel = panel.reshape(bcols, block_size, relations, width)
    partial_rows = aggregate_tile(
        blocks[0, 0], block_rows[0, 0], block_cols[0, 0], block_counts[0, 0], panel, brows
    )
    owned_sum = lax.psum_scatter(
        partial_rows.astype(jnp.bfloat16), "col", scatter_dimension=0, tiled=True
    ).astype(jnp.float32)
    self_term = jnp.dot(features, self_weight, preferred_element_type=jnp.float32)
    return jnp.maximum(self_term + owned_sum + bias, 0.0).astype(jnp.bfloat16)


def solution(mesh):
    return jax.shard_map(
        per_device,
        mesh=mesh,
        in_specs=(
            P(("row", "col"), None),
            P(),
            P(),
            P(),
            P("row", "col", None, None, None, None),
            P("row", "col", None, None),
            P("row", "col", None, None),
            P("row", "col", None),
        ),
        out_specs=P(("row", "col"), None),
        check_vma=False,
    )
```

profile of v0, /device:TPU:4, one launch (start us, length us, event | category | flops | bytes accessed | tf_op | source)
XLA Modules:
  0.0 435.1 jit_solution(4859910935213610332)
XLA Ops:
  6.5 9.1 %copy.23 = bf16[768,5,768]{0,2,1:T(8,128)(2,1)} copy(bf16[768,5,768]{2,0,1:T(8,128)(2,1)} %param.10) | data formatting | bytes 11796480 | tf_op args[2]
  15.7 5.7 %convolution_convert_fusion = bf16[128,3840]{1,0:T(8,128)(2,1)} fusion(bf16[128,768]{1,0:T(8,128)(2,1)S(1)} %copy-done.6, bf16[768,3840]{0,1:T(8,128)(2,1)} %bitcast.168), kind=kOutput, calls=%fused_computation.11 | convolution fusion | flops 755466240 | bytes 7077888 | tf_op jit(solution)/shard_map/dot_general | solution.py:40
  25.4 163.9 %all-gather.2.cloned.1.call-done = bf16[2048,3840]{1,0:T(8,128)(2,1)} async-done(((bf16[128,3840]{1,0:T(8,128)(2,1)}), bf16[2048,3840]{1,0:T(8,128)(2,1)}) %all-gather.2.cloned.1.call-update) | async-done | bytes 15728656 | tf_op jit(solution)/shard_map/all_gather | solution.py:41
  189.3 20.7 %copy.24 = bf16[2048,3840]{0,1:T(8,128)(2,1)} copy(bf16[2048,3840]{1,0:T(8,128)(2,1)} %all-gather.2.cloned.1.call-done) | data formatting | bytes 31457280 | tf_op jit(solution)/shard_map/all_gather | solution.py:41
  210.0 9.3 %copy.46 = bf16[480,8,16,128]{3,2,1,0:T(8,128)(2,1)S(1)} copy(bf16[480,8,16,128]{3,1,2,0:T(8,128)(2,1)} %bitcast.167) | data formatting | bytes 31457280
  219.3 5.9 %fusion.67 = (bf16[16,128,1,768]{1,0,3,2:T(8,128)(2,1)}, bf16[16,128,1,768]{1,0,3,2:T(8,128)(2,1)}, bf16[16,128,1,768]{1,0,3,2:T(8,128)(2,1)}, bf16[16,128,1,768]{1,0,3,2:T(8,128)(2,1)}, bf16[16,128,1,768]{1,0,3,2:T(8,128)(2,1)}) fusion(bf16[16,128,5,768]{1,0,3,2:T(8,128)(2,1)S(1)} %bitcast.166), kind=kLoop, calls=%fused_computation.110 | loop fusion | bytes 31457280 | tf_op jit(solution)/shard_map/slice | solution.py:14
  225.2 5.0 %copy.34 = bf16[16,128,1,768]{3,1,0,2:T(8,128)(2,1)} copy(bf16[16,128,1,768]{1,0,3,2:T(8,128)(2,1)} %get-tuple-element.6) | data formatting | bytes 6291456 | tf_op jit(solution)/shard_map/slice | solution.py:14
  237.1 5.0 %copy.31 = bf16[16,128,1,768]{3,1,0,2:T(8,128)(2,1)} copy(bf16[16,128,1,768]{1,0,3,2:T(8,128)(2,1)} %get-tuple-element.7) | data formatting | bytes 6291456 | tf_op jit(solution)/shard_map/slice | solution.py:14
  249.2 5.1 %copy.25 = bf16[16,128,1,768]{3,1,0,2:T(8,128)(2,1)} copy(bf16[16,128,1,768]{1,0,3,2:T(8,128)(2,1)} %get-tuple-element.9) | data formatting | bytes 6291456 | tf_op jit(solution)/shard_map/slice | solution.py:14
  261.2 5.0 %copy.28 = bf16[16,128,1,768]{3,1,0,2:T(8,128)(2,1)} copy(bf16[16,128,1,768]{1,0,3,2:T(8,128)(2,1)} %get-tuple-element.8) | data formatting | bytes 6291456 | tf_op jit(solution)/shard_map/slice | solution.py:14
  273.3 5.0 %copy.37 = bf16[16,128,1,768]{3,1,0,2:T(8,128)(2,1)} copy(bf16[16,128,1,768]{1,0,3,2:T(8,128)(2,1)} %get-tuple-element.5) | data formatting | bytes 6291456 | tf_op jit(solution)/shard_map/slice | solution.py:14
  290.6 4.1 convert_reduce_fusion.2
  294.7 2.9 copy.33
  297.6 4.1 convert_reduce_fusion.4
  301.8 3.0 copy.27
  304.8 4.1 convert_reduce_fusion.3
  308.9 3.0 copy.30
  311.9 4.2 convert_reduce_fusion
  316.0 3.0 copy.39
  321.8 3.4 fusion.35
  325.2 3.4 fusion.39
  328.6 7.3 %add_convert_fusion = bf16[16,128,768]{2,0,1:T(8,128)(2,1)S(1)} fusion(f32[16,128,768]{2,0,1:T(8,128)S(1)} %fusion.47, f32[16,128,768]{2,0,1:T(8,128)S(1)} %fusion.43, f32[16,128,768]{2,0,1:T(8,128)} %fusion.35, f32[16,128,768]{2,0,1:T(8,128)} %fusion.39, bf16[8,128,768]{2,0,1:T(8,128)(2,1)} %copy.39, s32[8]{0:T(128)S(1)} %get-tuple-element.10, ...), kind=kOutput, calls=%fused_computation.5 | convolution fusion | flops 33030400 | bytes 29884456 | tf_op jit(solution)/shard_map/ns,shid->nid/dot_general | solution.py:26
  336.0 2.7 copy.40
  338.7 87.6 %reduce-scatter.2.cloned.1.call-done = bf16[128,768]{1,0:T(8,128)(2,1)} async-done(((bf16[2048,768]{1,0:T(8,128)(2,1)}), bf16[128,768]{1,0:T(8,128)(2,1)}) %reduce-scatter.2.cloned.1.call-update) | async-done | bytes 196624 | tf_op jit(solution)/shard_map/reduce_scatter | solution.py:46
  (62 shorter events, 48.8 us)
Async XLA Ops:
  6.5 419.8 %copy-start = (bf16[768,768]{1,0:T(8,128)(2,1)S(1)}, bf16[768,768]{1,0:T(8,128)(2,1)}, u32[]{:S(2)}) copy-start(bf16[768,768]{1,0:T(8,128)(2,1)} %param.9) | copy-start | bytes 3538948
  6.5 9.1 %copy-start.6 = (bf16[128,768]{1,0:T(8,128)(2,1)S(1)}, bf16[128,768]{1,0:T(8,128)(2,1)}, u32[]{:S(2)}) copy-start(bf16[128,768]{1,0:T(8,128)(2,1)} %param.8) | copy-start | bytes 589828
  6.5 182.7 %all-gather.2.cloned.1.call-start = ((), (), s32[]{:S(2)}) async-start(), calls=%async_computation.1 | async-start | bytes 16711680 | tf_op jit(solution)/shard_map/all_gather | solution.py:41
  15.7 5.8 %copy-start.7 = (s32[1,1,5]{2,1,0:T(1,128)S(1)}, s32[1,1,5]{2,1,0:T(1,128)}, u32[]{:S(2)}) copy-start(s32[1,1,5]{2,1,0:T(1,128)} %param.15) | copy-start | bytes 64
  15.7 9.6 %copy-start.9 = (s32[1,1,5,8]{3,1,2,0:T(1,128)S(1)}, s32[1,1,5,8]{3,1,2,0:T(1,128)}, u32[]{:S(2)}) copy-start(s32[1,1,5,8]{3,1,2,0:T(1,128)} %param.14) | copy-start | bytes 484
  15.7 9.7 %copy-start.10 = (s32[1,1,5,8]{3,1,2,0:T(1,128)S(1)}, s32[1,1,5,8]{3,1,2,0:T(1,128)}, u32[]{:S(2)}) copy-start(s32[1,1,5,8]{3,1,2,0:T(1,128)} %param.13) | copy-start | bytes 484
  21.4 405.0 %reduce-scatter.2.cloned.1.call-start = ((), (), s32[]{:S(2)}) async-start(), calls=%async_computation.2 | async-start | bytes 3342336 | tf_op jit(solution)/shard_map/reduce_scatter | solution.py:46
  283.9 1.9 copy-start.4
  283.9 2.4 copy-start.5
  319.0 1.4 copy-start.1
  320.4 1.4 copy-start.2
  321.8 3.4 copy-start.3
  338.7 87.7 %copy-start.8 = (f32[768]{0:T(1024)S(1)}, f32[768]{0:T(1024)}, u32[]{:S(2)}) copy-start(f32[768]{0:T(1024)} %param.11) | copy-start | bytes 9220
Sparse Core Ops, SparseCore 0:
  21.5 167.6 all-gather.1
  338.9 87.4 reduce-scatter.1
where the time goes:
time: 437 us; the launch traced here: 435 us
  waiting for transfers between devices  252 us (58%)
  local copies, waits for them, and re-layouts  102 us (23%)
  other arithmetic  35.8 us (8%)
  matrix products  31.9 us (7%)
  between operations  13.6 us (3%)
    all_gather x1, waiting for transfers between devices, per_device(): panel = lax.all_gather(own_rows, 'row', axis=0, tiled=True)  164 us
    reduce_scatter x1, waiting for transfers between devices, per_device(): lax.psum_scatter(partial_rows.astype(jnp.bfloat16), 'col', scatter_dimens...  87.6 us
    slice x6, local copies, waits for them, and re-layouts, aggregate_tile(): source = panel[:, :, relation, :]  31 us
    all_gather x1, local copies, waits for them, and re-layouts, per_device(): panel = lax.all_gather(own_rows, 'row', axis=0, tiled=True)  20.7 us
    unnamed x24, local copies, waits for them, and re-layouts  20.1 us
    reduce_sum x5, other arithmetic, aggregate_tile(): jnp.einsum('ns,shid->nid', owners, halves, preferred_element_type=jnp.flo...  18.4 us
    dot_general x5, matrix products, aggregate_tile(): jnp.einsum('ns,shid->nid', owners, halves, preferred_element_type=jnp.flo...  16.3 us
    another operation x10, other arithmetic, aggregate_tile(): halves = jnp.stack([upper, lower], axis=1)  14.3 us
  transfers between devices with their start and end apart: 2, of which 2 were waited for; matrix products, arithmetic and copies ran while one was open for 1% of the time, Pallas kernels for 0%

commit v1 on v0

v1 whole, which is shorter than its diff:
```python
import functools

import jax
import jax.numpy as jnp
from jax import lax
from jax.experimental import pallas as pl
from jax.experimental.pallas import tpu as pltpu
from jax.sharding import PartitionSpec as P


def tile_kernel(
    slots, rows_ref, cols_ref, counts_ref, blocks_ref, panel_ref, weight_ref, out_ref, total, picked
):
    relations = weight_ref.shape[0]
    size = blocks_ref.shape[-1]
    total[...] = jnp.zeros_like(total)
    for relation in range(relations):
        live = counts_ref[relation]

        def pick(slot, carry):
            at = relation * slots + slot
            source = pl.multiple_of(cols_ref[at] * size, size)
            product = jnp.dot(
                blocks_ref[at], panel_ref[pl.ds(source, size), :], preferred_element_type=jnp.float32
            )
            picked[pl.ds(pl.multiple_of(slot * size, size), size), :] = product.astype(picked.dtype)
            return carry

        lax.fori_loop(0, live, pick, 0)

        def spread(pair, carry):
            first = pl.multiple_of(pair * 2 * size, 2 * size)
            moved = jnp.dot(
                picked[pl.ds(first, 2 * size), :],
                weight_ref[relation],
                preferred_element_type=jnp.float32,
            )
            for half in range(2):
                slot = pair * 2 + half

                @pl.when(slot < live)
                def _():
                    target = pl.multiple_of(rows_ref[relation * slots + slot] * size, size)
                    total[pl.ds(target, size), :] += moved[half * size : (half + 1) * size]

            return carry

        lax.fori_loop(0, (live + 1) // 2, spread, 0)
    out_ref[...] = total[...].astype(out_ref.dtype)


def aggregate_tile(tile_blocks, tile_rows, tile_cols, tile_counts, panel, weights, brows):
    relations, slots, size, _ = tile_blocks.shape
    width = panel.shape[-1]
    vmem = pl.BlockSpec(memory_space=pltpu.VMEM)
    smem = pl.BlockSpec(memory_space=pltpu.SMEM)
    return pl.pallas_call(
        functools.partial(tile_kernel, slots),
        out_shape=jax.ShapeDtypeStruct((brows * size, width), jnp.bfloat16),
        in_specs=[smem, smem, smem, vmem, vmem, vmem],
        out_specs=vmem,
        scratch_shapes=[
            pltpu.VMEM((brows * size, width), jnp.float32),
            pltpu.VMEM((slots * size, width), jnp.bfloat16),
        ],
        compiler_params=pltpu.CompilerParams(vmem_limit_bytes=32 << 20),
        name="tile",
    )(
        tile_rows.reshape(-1),
        tile_cols.reshape(-1),
        tile_counts,
        tile_blocks.reshape(relations * slots, size, size),
        panel,
        weights,
    )


def per_device(
    features, self_weight, rel_weight, bias, blocks, block_rows, block_cols, block_counts
):
    rows_dev, width = features.shape
    size = blocks.shape[-1]
    brows = rows_dev * lax.axis_size("col") // size
    weights = jnp.transpose(rel_weight, (1, 0, 2))
    panel = lax.all_gather(features, "row", axis=0, tiled=True)
    partial_rows = aggregate_tile(
        blocks[0, 0], block_rows[0, 0], block_cols[0, 0], block_counts[0, 0], panel, weights, brows
    )
    owned_sum = lax.psum_scatter(partial_rows, "col", scatter_dimension=0, tiled=True)
    self_term = jnp.dot(features, self_weight, preferred_element_type=jnp.float32)
    return jnp.maximum(self_term + owned_sum.astype(jnp.float32) + bias, 0.0).astype(jnp.bfloat16)


def solution(mesh):
    return jax.shard_map(
        per_device,
        mesh=mesh,
        in_specs=(
            P(("row", "col"), None),
            P(),
            P(),
            P(),
            P("row", "col", None, None, None, None),
            P("row", "col", None, None),
            P("row", "col", None, None),
            P("row", "col", None),
        ),
        out_specs=P(("row", "col"), None),
        check_vma=False,
    )
```

time: 437 us -> 201 us (0.46)
  local copies, waits for them, and re-layouts: 102 us -> 8.35 us
  waiting for transfers between devices: 252 us -> 167 us
  other arithmetic: 35.8 us -> 1.4 us
  matrix products: 31.9 us -> 1.94 us
  Pallas kernels: 0 us -> 7.97 us
    all_gather x1, waiting for transfers between devices: 164 us -> 72.9 us  [per_device(): panel = lax.all_gather(features, 'row', axis=0, tiled=True)]
    slice x7 -> x0, local copies, waits for them, and re-layouts: 31.7 us -> none  [the longest x6 31 us: aggregate_tile(): source = panel[:, :, relation, :]]
    dot_general x11 -> x0, matrix products: 30 us -> none  [the longest x5 16.3 us: aggregate_tile(): jnp.einsum('ns,shid->nid', owners, halves, preferred_element_type=jnp.flo...]
    all_gather x1 -> x0, local copies, waits for them, and re-layouts: 20.7 us -> none  [per_device(): panel = lax.all_gather(own_rows, 'row', axis=0, tiled=True)]
    reduce_sum x5 -> x0, other arithmetic: 18.4 us -> none  [aggregate_tile(): jnp.einsum('ns,shid->nid', owners, halves, preferred_element_type=jnp.flo...]
    another operation x10 -> x0, other arithmetic: 14.3 us -> none  [aggregate_tile(): halves = jnp.stack([upper, lower], axis=1)]
    reduce_sum x5 -> x0, local copies, waits for them, and re-layouts: 14.3 us -> none  [aggregate_tile(): jnp.einsum('ns,shid->nid', owners, halves, preferred_element_type=jnp.flo...]
    gather x5 -> x0, local copies, waits for them, and re-layouts: 12.7 us -> none  [aggregate_tile(): chosen = source[tile_cols[relation]]]
where the time goes in v1:
time: 201 us; the launch traced here: 200 us
  waiting for transfers between devices  167 us (83%)
  between operations  13.4 us (7%)
  local copies, waits for them, and re-layouts  8.35 us (4%)
  Pallas kernels  7.97 us (4%)
    reduce_scatter x1, waiting for transfers between devices, per_device(): lax.psum_scatter(partial_rows, 'col', scatter_dimension=0, tiled=True)  93.4 us
    all_gather x1, waiting for transfers between devices, per_device(): panel = lax.all_gather(features, 'row', axis=0, tiled=True)  72.9 us
    unnamed x16, local copies, waits for them, and re-layouts  8.19 us
    pallas_call x1, Pallas kernels, aggregate_tile(): pl.pallas_call(functools.partial(tile_kernel, slots), out_shape=jax.Shape...  7.97 us
  transfers between devices with their start and end apart: 2, of which 2 were waited for; matrix products, arithmetic and copies ran while one was open for 1% of the time, Pallas kernels for 0%

profile of v1, /device:TPU:4, one launch (start us, length us, event | category | flops | bytes accessed | tf_op | source)
XLA Modules:
  0.0 200.1 jit_solution(7536770006934136185)
XLA Ops:
  6.5 0.0 copy-start
  6.5 0.0 all-gather.2.cloned.1.call-start
  6.5 0.7 all-gather.2.cloned.1.call-update
  7.3 0.0 reduce-scatter.2.cloned.1.call-start
  7.3 0.7 reduce
  8.0 0.1 reshape_squeeze.9.rows_ref
  8.1 0.7 reduce.1
  8.8 0.1 reshape_squeeze.10.cols_ref
  8.9 72.9 %all-gather.2.cloned.1.call-done.panel_ref = bf16[2048,768]{1,0:T(8,128)(2,1)} async-done(((bf16[128,768]{1,0:T(8,128)(2,1)}), bf16[2048,768]{1,0:T(8,128)(2,1)}) %all-gather.2.cloned.1.call-update) | async-done | bytes 3145744 | tf_op jit(solution)/shard_map/all_gather | solution.py:85
  81.8 0.0 copy-start.2
  81.8 2.7 %copy-done.2 = bf16[768,5,768]{2,0,1:T(8,128)(2,1)S(1)} copy-done((bf16[768,5,768]{2,0,1:T(8,128)(2,1)S(1)}, bf16[768,5,768]{2,0,1:T(8,128)(2,1)}, u32[]{:S(2)}) %copy-start.2) | copy-done | bytes 5898264
  84.4 0.0 copy-start.3
  84.4 1.9 copy-done.3
  86.3 1.3 copy-done.4
  87.6 0.7 copy-done.5
  88.3 8.0 %tile.1 = bf16[2048,768]{1,0:T(8,128)(2,1)S(1)} custom-call(s32[40]{0:T(128)S(1)} %reshape_squeeze.9.rows_ref, s32[40]{0:T(128)S(1)} %reshape_squeeze.10.cols_ref, s32[5]{0:T(128)S(1)} %bitcast.7, bf16[40,128,128]{2,1,0:T(8,128)(2,1)S(1)} %bitcast.6, bf16[2048,768]{1,0:T(8,128)(2,1)S(1)} %copy-done.3, bf16[5,768,768]{2,1,0:T(8,128)(2,1)S(1)} %bitcast.5), custom_call_target="tpu_custom_call" | custom-call | tf_op jit(solution)/shard_map/tile/pallas_call | solution.py:57
  96.3 0.0 copy-start.1
  96.3 1.6 copy-done.1
  97.9 0.0 reduce-scatter.2.cloned.1.call-update
  98.0 93.4 %reduce-scatter.2.cloned.1.call-done = bf16[128,768]{1,0:T(8,128)(2,1)} async-done(((bf16[2048,768]{1,0:T(8,128)(2,1)}), bf16[128,768]{1,0:T(8,128)(2,1)}) %reduce-scatter.2.cloned.1.call-update) | async-done | bytes 196624 | tf_op jit(solution)/shard_map/reduce_scatter | solution.py:89
  191.4 0.0 copy-done
  191.4 0.0 copy-done.6
  191.4 0.0 copy-done.7
  191.4 1.9 fusion.2
  (4 shorter events, 0.0 us)
Async XLA Ops:
  6.5 184.8 %copy-start = (bf16[768,768]{1,0:T(8,128)(2,1)S(1)}, bf16[768,768]{1,0:T(8,128)(2,1)}, u32[]{:S(2)}) copy-start(bf16[768,768]{1,0:T(8,128)(2,1)} %param.9) | copy-start | bytes 3538948
  6.5 75.2 %all-gather.2.cloned.1.call-start = ((), (), s32[]{:S(2)}) async-start(), calls=%async_computation.1 | async-start | bytes 3342336 | tf_op jit(solution)/shard_map/all_gather | solution.py:85
  7.3 184.1 %reduce-scatter.2.cloned.1.call-start = ((), (), s32[]{:S(2)}) async-start(), calls=%async_computation.2 | async-start | bytes 3342336 | tf_op jit(solution)/shard_map/reduce_scatter | solution.py:89
  81.8 2.7 %copy-start.2 = (bf16[768,5,768]{2,0,1:T(8,128)(2,1)S(1)}, bf16[768,5,768]{2,0,1:T(8,128)(2,1)}, u32[]{:S(2)}) copy-start(bf16[768,5,768]{2,0,1:T(8,128)(2,1)} %param.10) | copy-start | bytes 17694724
  84.4 1.9 copy-start.3
  86.3 1.3 copy-start.4
  87.6 0.7 copy-start.5
  96.3 1.7 copy-start.1
  97.9 93.4 %copy-start.6 = (bf16[128,768]{1,0:T(8,128)(2,1)S(1)}, bf16[128,768]{1,0:T(8,128)(2,1)}, u32[]{:S(2)}) copy-start(bf16[128,768]{1,0:T(8,128)(2,1)} %param.8) | copy-start | bytes 589828
  97.9 93.4 %copy-start.7 = (f32[768]{0:T(1024)S(1)}, f32[768]{0:T(1024)}, u32[]{:S(2)}) copy-start(f32[768]{0:T(1024)} %param.11) | copy-start | bytes 9220
Sparse Core Ops, SparseCore 0:
  10.1 71.6 all-gather.1
  98.1 93.2 reduce-scatter.1

commit v2 on v1

v2 whole, which is shorter than its diff:
```python
import functools

import jax
import jax.numpy as jnp
from jax import lax
from jax.experimental import pallas as pl
from jax.experimental.pallas import tpu as pltpu
from jax.sharding import PartitionSpec as P

X, CORES, Z, Y = 4, 2, 4, 4
SPLIT = 512


def row_shift(value, dz, dx, dc):
    pairs = []
    for index in range(16):
        z, x, c = index // 8, index // 2 % 4, index % 2
        pairs.append((index, (z ^ dz) * 8 + (x + dx) % X * 2 + (c ^ dc)))
    return lax.ppermute(value, "row", pairs)


def col_shift(value, dz, dy):
    pairs = []
    for index in range(16):
        z, y = index // 4, index % 4
        pairs.append((index, (z + dz) % Z * 4 + (y + dy) % Y))
    return lax.ppermute(value, "col", pairs)


def tile_kernel(
    slots, rows_ref, cols_ref, counts_ref, blocks_ref, weight_ref, *rest
):
    group_refs, y_refs, z_refs, (total, picked) = rest[:4], rest[4:8], rest[8:12], rest[12:]
    relations = weight_ref.shape[0]
    size = blocks_ref.shape[-1]
    total[...] = jnp.zeros_like(total)
    for relation in range(relations):
        live = counts_ref[relation]

        def pick(slot, carry):
            at = relation * slots + slot
            place = cols_ref[at]
            source = pl.multiple_of(place % 4 * size, size)
            out_rows = pl.ds(pl.multiple_of(slot * size, size), size)
            for group, group_ref in enumerate(group_refs):

                @pl.when(place // 4 == group)
                def _():
                    product = jnp.dot(
                        blocks_ref[at],
                        group_ref[pl.ds(source, size), :],
                        preferred_element_type=jnp.float32,
                    )
                    picked[out_rows, :] = product.astype(picked.dtype)

            return carry

        lax.fori_loop(0, live, pick, 0)

        def spread(pair, carry):
            first = pl.multiple_of(pair * 2 * size, 2 * size)
            moved = jnp.dot(
                picked[pl.ds(first, 2 * size), :],
                weight_ref[relation],
                preferred_element_type=jnp.float32,
            )
            for half in range(2):
                slot = pair * 2 + half

                @pl.when(slot < live)
                def _():
                    target = pl.multiple_of(rows_ref[relation * slots + slot] * size, size)
                    total[pl.ds(target, size), :] += moved[half * size : (half + 1) * size]

            return carry

        lax.fori_loop(0, (live + 1) // 2, spread, 0)
    for d in range(Y):
        for e in range(Z):
            rows = pl.ds((d * Z + e) * size, size)
            y_refs[d][e] = total[rows, :SPLIT].astype(jnp.bfloat16)
            z_refs[e][d] = total[rows, SPLIT:].astype(jnp.bfloat16)


def merge_kernel(own_ref, *refs):
    ins, (keep_ref, *send_refs) = refs[:3], refs[3:]
    for e in range(len(send_refs) + 1):
        summed = own_ref[e].astype(jnp.float32)
        for ref in ins:
            summed += ref[e].astype(jnp.float32)
        if e == 0:
            keep_ref[...] = summed
        else:
            send_refs[e - 1][...] = summed.astype(jnp.bfloat16)


def merge(own, ins):
    vmem = pl.BlockSpec(memory_space=pltpu.VMEM)
    count, rows, columns = own.shape
    return pl.pallas_call(
        merge_kernel,
        out_shape=[jax.ShapeDtypeStruct((rows, columns), jnp.float32)]
        + [jax.ShapeDtypeStruct((rows, columns), jnp.bfloat16)] * (count - 1),
        in_specs=[vmem] * 4,
        out_specs=[vmem] * count,
        compiler_params=pltpu.CompilerParams(vmem_limit_bytes=4 << 20),
        name="merge",
    )(own, *ins)


def aggregate_tile(tile_blocks, tile_rows, tile_cols, tile_counts, groups, weights):
    relations, slots, size, _ = tile_blocks.shape
    width = weights.shape[-1]
    vmem = pl.BlockSpec(memory_space=pltpu.VMEM)
    smem = pl.BlockSpec(memory_space=pltpu.SMEM)
    y_shape = jax.ShapeDtypeStruct((Z, size, SPLIT), jnp.bfloat16)
    z_shape = jax.ShapeDtypeStruct((Y, size, width - SPLIT), jnp.bfloat16)
    outs = pl.pallas_call(
        functools.partial(tile_kernel, slots),
        out_shape=[y_shape] * Y + [z_shape] * Z,
        in_specs=[smem] * 3 + [vmem] * 6,
        out_specs=[vmem] * (Y + Z),
        scratch_shapes=[
            pltpu.VMEM((Y * Z * size, width), jnp.float32),
            pltpu.VMEM((slots * size, width), jnp.bfloat16),
        ],
        compiler_params=pltpu.CompilerParams(vmem_limit_bytes=32 << 20),
        name="tile",
    )(
        tile_rows.reshape(-1),
        tile_cols.reshape(-1),
        tile_counts,
        tile_blocks.reshape(relations * slots, size, size),
        weights,
        *groups,
    )
    return outs[:Y], outs[Y:]


def gather_groups(features, self_term):
    far = row_shift(features, 1, 0, 0)
    near_parts = [features] + [row_shift(features, 0, d, 0) for d in (1, 3, 2)]
    far, self_term = lax.optimization_barrier((far, self_term))
    far_parts = [far] + [row_shift(far, 0, d, 0) for d in (1, 3, 2)]
    near = jnp.concatenate(near_parts, axis=0)
    near_other = row_shift(near, 0, 0, 1)
    rest = jnp.concatenate(far_parts, axis=0)
    rest_other = row_shift(rest, 0, 0, 1)
    return (near, rest, near_other, rest_other), self_term


def panel_place(source, me):
    z, x, c = source // 8 ^ me // 8, (me // 2 - source // 2) % X, source % 2 ^ me % 2
    place = jnp.where(x == 2, 3, jnp.where(x == 3, 2, x))
    return c * 8 + z * 4 + place


def scatter_sum(y_parts, z_parts):
    y_in = [col_shift(y_parts[d], 0, d) for d in (1, 3, 2)]
    z_in = [col_shift(z_parts[e], e, 0) for e in (1, 3, 2)]
    z_own, *z_send = merge(z_parts[0], z_in)
    y_own, *y_send = merge(y_parts[0], y_in)
    z_last = [col_shift(z_send[d - 1], 0, d) for d in (1, 3, 2)]
    y_last = [col_shift(y_send[e - 1], e, 0) for e in (1, 3, 2)]
    y_own += sum(part.astype(jnp.float32) for part in y_last)
    z_own += sum(part.astype(jnp.float32) for part in z_last)
    return y_own, z_own


def per_device(
    features, self_weight, rel_weight, bias, blocks, block_rows, block_cols, block_counts
):
    row_me, col_me = lax.axis_index("row"), lax.axis_index("col")
    weights = jnp.transpose(rel_weight, (1, 0, 2))
    targets = (block_rows[0, 0] % Y - col_me % Y) % Y * Z + (block_rows[0, 0] // Y - col_me // Y) % Z
    sources = panel_place(block_cols[0, 0], row_me)
    self_term = jnp.dot(features, self_weight, preferred_element_type=jnp.float32) + bias
    groups, self_term = gather_groups(features, self_term)
    y_parts, z_parts = aggregate_tile(
        blocks[0, 0], targets, sources, block_counts[0, 0], groups, weights
    )
    y_own, z_own = scatter_sum(y_parts, z_parts)
    owned = jnp.concatenate([y_own, z_own], axis=1)
    return jnp.maximum(self_term + owned, 0.0).astype(jnp.bfloat16)


def solution(mesh):
    return jax.shard_map(
        per_device,
        mesh=mesh,
        in_specs=(
            P(("row", "col"), None),
            P(),
            P(),
            P(),
            P("row", "col", None, None, None, None),
            P("row", "col", None, None),
            P("row", "col", None, None),
            P("row", "col", None),
        ),
        out_specs=P(("row", "col"), None),
        check_vma=False,
    )
```

time: 201 us -> 97.5 us (0.49)
  waiting for transfers between devices: 167 us -> 38 us
  starting transfers between devices: 0.04 us -> 39.5 us
  between operations: 13.4 us -> 0.19 us
  Pallas kernels: 7.97 us -> 11.7 us
  local copies, waits for them, and re-layouts: 8.35 us -> 5.69 us
    reduce_scatter x1 -> x0, waiting for transfers between devices: 93.4 us -> none  [per_device(): lax.psum_scatter(partial_rows, 'col', scatter_dimension=0, tiled=True)]
    all_gather x1 -> x0, waiting for transfers between devices: 72.9 us -> none  [per_device(): panel = lax.all_gather(features, 'row', axis=0, tiled=True)]
    ppermute x0 -> x21, starting transfers between devices: none -> 39.5 us  [the longest x12 25.1 us: col_shift(): return lax.ppermute(value, 'col', pairs)]
    ppermute x0 -> x21, waiting for transfers between devices: none -> 38 us  [the longest x12 27.8 us: col_shift(): return lax.ppermute(value, 'col', pairs)]
    pallas_call x1 -> x3, Pallas kernels: 7.97 us -> 11.7 us  [the longest x1 11.3 us: aggregate_tile(): pl.pallas_call(functools.partial(tile_kernel, slots), out_shape=[y_shape]...]
    unnamed x16 -> x22, local copies, waits for them, and re-layouts: 8.19 us -> 4.84 us
  transfers between devices with their start and end apart: 2 -> 21, of which waited for: 2 -> 8; matrix products, arithmetic and copies ran while one was open for 1% -> 5% of each run, Pallas kernels for 0% -> 0%
where the time goes in v2:
time: 97.5 us; the launch traced here: 98 us
  starting transfers between devices  39.5 us (41%)
  waiting for transfers between devices  38 us (39%)
  Pallas kernels  11.7 us (12%)
  local copies, waits for them, and re-layouts  5.69 us (6%)
  matrix products  2.06 us (2%)
    ppermute x12, waiting for transfers between devices, col_shift(): return lax.ppermute(value, 'col', pairs)  27.8 us
    ppermute x12, starting transfers between devices, col_shift(): return lax.ppermute(value, 'col', pairs)  25.1 us
    ppermute x9, starting transfers between devices, row_shift(): return lax.ppermute(value, 'row', pairs)  14.4 us
    pallas_call x1, Pallas kernels, aggregate_tile(): pl.pallas_call(functools.partial(tile_kernel, slots), out_shape=[y_shape]...  11.3 us
    ppermute x9, waiting for transfers between devices, row_shift(): return lax.ppermute(value, 'row', pairs)  10.2 us
    unnamed x22, local copies, waits for them, and re-layouts  4.84 us
    dot_general x1, matrix products, per_device(): jnp.dot(features, self_weight, preferred_element_type=jnp.float32) + bias  2.06 us
  transfers between devices with their start and end apart: 21, of which 8 were waited for; matrix products, arithmetic and copies ran while one was open for 5% of the time, Pallas kernels for 0%

profile of v2, /device:TPU:4, one launch (start us, length us, event | category | flops | bytes accessed | tf_op | source)
XLA Modules:
  0.0 98.0 jit_solution(2873123555324114545)
XLA Ops:
  0.5 1.5 %collective-permute-start.1 = (bf16[128,768]{1,0:T(8,128)(2,1)}, bf16[128,768]{1,0:T(8,128)(2,1)S(1)}, u32[]{:S(2)}, u32[]{:S(2)}) collective-permute-start(bf16[128,768]{1,0:T(8,128)(2,1)} %param.8), channel_id=1, source_target_pairs={{0,32},{16,48},{32,64},{48,80},{64,96},{80,112},{96,0},{112,16},{1... | collective-permute-start | bytes 589832 | tf_op jit(solution)/shard_map/ppermute | solution.py:19
  2.0 7.2 %collective-permute-start = (bf16[128,768]{1,0:T(8,128)(2,1)}, bf16[128,768]{1,0:T(8,128)(2,1)S(1)}, u32[]{:S(2)}, u32[]{:S(2)}) collective-permute-start(bf16[128,768]{1,0:T(8,128)(2,1)} %param.8), channel_id=1, source_target_pairs={{0,128},{16,144},{32,160},{48,176},{64,192},{80,208},{96,224},{112... | collective-permute-start | bytes 589832 | tf_op jit(solution)/shard_map/ppermute | solution.py:19
  9.2 1.2 %collective-permute-start.3 = (bf16[128,768]{1,0:T(8,128)(2,1)}, bf16[128,768]{1,0:T(8,128)(2,1)S(1)}, u32[]{:S(2)}, u32[]{:S(2)}) collective-permute-start(bf16[128,768]{1,0:T(8,128)(2,1)} %param.8), channel_id=1, source_target_pairs={{0,64},{16,80},{32,96},{48,112},{64,0},{80,16},{96,32},{112,48},{1... | collective-permute-start | bytes 589832 | tf_op jit(solution)/shard_map/ppermute | solution.py:19
  10.5 2.1 %convolution_add_fusion = f32[128,768]{1,0:T(8,128)} fusion(bf16[128,768]{1,0:T(8,128)(2,1)} %param.8, bf16[768,768]{1,0:T(8,128)(2,1)S(1)} %copy-done, f32[768]{0:T(1024)} %param.11), kind=kOutput, calls=%fused_computation | convolution fusion | flops 151093248 | bytes 1772544 | tf_op jit(solution)/shard_map/dot_general | solution.py:177
  12.5 1.4 %collective-permute-done = bf16[128,768]{1,0:T(8,128)(2,1)S(1)} collective-permute-done((bf16[128,768]{1,0:T(8,128)(2,1)}, bf16[128,768]{1,0:T(8,128)(2,1)S(1)}, u32[]{:S(2)}, u32[]{:S(2)}) %collective-permute-start) | collective-permute-done | bytes 196640 | tf_op jit(solution)/shard_map/ppermute | solution.py:19
  13.9 1.6 %collective-permute-start.6 = (bf16[128,768]{1,0:T(8,128)(2,1)S(1)}, bf16[128,768]{1,0:T(8,128)(2,1)S(1)}, u32[]{:S(2)}, u32[]{:S(2)}) collective-permute-start(bf16[128,768]{1,0:T(8,128)(2,1)S(1)} %collective-permute-done), channel_id=1, source_target_pairs={{0,64},{16,80},{32,96},{48,112},{64,0},{80,16},{96,32},{112,48},{1... | collective-permute-start | bytes 589832 | tf_op jit(solution)/shard_map/ppermute | solution.py:19
  15.5 2.3 %collective-permute-start.5 = (bf16[128,768]{1,0:T(8,128)(2,1)S(1)}, bf16[128,768]{1,0:T(8,128)(2,1)S(1)}, u32[]{:S(2)}, u32[]{:S(2)}) collective-permute-start(bf16[128,768]{1,0:T(8,128)(2,1)S(1)} %collective-permute-done), channel_id=1, source_target_pairs={{0,96},{16,112},{32,0},{48,16},{64,32},{80,48},{96,64},{112,80},{1... | collective-permute-start | bytes 589832 | tf_op jit(solution)/shard_map/ppermute | solution.py:19
  18.7 6.5 %collective-permute-done.4 = bf16[128,768]{1,0:T(8,128)(2,1)S(1)} collective-permute-done((bf16[128,768]{1,0:T(8,128)(2,1)S(1)}, bf16[128,768]{1,0:T(8,128)(2,1)S(1)}, u32[]{:S(2)}, u32[]{:S(2)}) %collective-permute-start.4) | collective-permute-done | bytes 196640 | tf_op jit(solution)/shard_map/ppermute | solution.py:19
  25.2 0.7 constant_dynamic-update-slice_fusion.6
  27.5 2.4 %collective-permute-done.8.rest_3_ = bf16[512,768]{1,0:T(8,128)(2,1)} collective-permute-done((bf16[512,768]{1,0:T(8,128)(2,1)}, bf16[512,768]{1,0:T(8,128)(2,1)}, u32[]{:S(2)}, u32[]{:S(2)}) %collective-permute-start.8) | collective-permute-done | bytes 786464 | tf_op jit(solution)/shard_map/ppermute | solution.py:19
  29.9 2.7 %copy-done.1 = bf16[768,5,768]{2,0,1:T(8,128)(2,1)S(1)} copy-done((bf16[768,5,768]{2,0,1:T(8,128)(2,1)S(1)}, bf16[768,5,768]{2,0,1:T(8,128)(2,1)}, u32[]{:S(2)}) %copy-start.1) | copy-done | bytes 5898264
  32.6 11.3 %tile.1 = (bf16[4,128,512]{2,1,0:T(8,128)(2,1)S(1)}, bf16[4,128,512]{2,1,0:T(8,128)(2,1)S(1)}, bf16[4,128,512]{2,1,0:T(8,128)(2,1)S(1)}, bf16[4,128,512]{2,1,0:T...) custom-call(s32[40]{0:T(128)S(1)} %get-tuple-element.41.rows_ref, ...), custom_call_target="tpu_custom_call" | custom-call | tf_op jit(solution)/shard_map/tile/pallas_call | solution.py:118
  43.9 8.0 %collective-permute-start.15 = (bf16[4,128,256]{2,1,0:T(8,128)(2,1)S(1)}, bf16[4,128,256]{2,1,0:T(8,128)(2,1)S(1)}, u32[]{:S(2)}, u32[]{:S(2)}) collective-permute-start(bf16[4,128,256]{2,1,0:T(8,128)(2,1)S(1)} %get-tuple-element.34), channel_id=1, source_target_pairs={{0,4},{1,5},{2,6},{3,7},{4,8},{5,9},{6,10},{7,11},{8,12},{9,13},{1... | collective-permute-start | bytes 786440 | tf_op jit(solution)/shard_map/ppermute | solution.py:27
  51.9 3.2 %collective-permute-start.10 = (bf16[4,128,512]{2,1,0:T(8,128)(2,1)S(1)}, bf16[4,128,512]{2,1,0:T(8,128)(2,1)S(1)}, u32[]{:S(2)}, u32[]{:S(2)}) collective-permute-start(bf16[4,128,512]{2,1,0:T(8,128)(2,1)S(1)} %get-tuple-element.27), channel_id=1, source_target_pairs={{0,3},{1,0},{2,1},{3,2},{4,7},{5,4},{6,5},{7,6},{8,11},{9,8},{10,9... | collective-permute-start | bytes 1572872 | tf_op jit(solution)/shard_map/ppermute | solution.py:27
  55.2 1.3 %collective-permute-done.15.refs_0_ = bf16[4,128,256]{2,1,0:T(8,128)(2,1)S(1)} collective-permute-done((bf16[4,128,256]{2,1,0:T(8,128)(2,1)S(1)}, bf16[4,128,256]{2,1,0:T(8,128)(2,1)S(1)}, u32[]{:S(2)}, u32[]{:S(2)}) %collective-permute-start.15) | collective-permute-done | bytes 262176 | tf_op jit(solution)/shard_map/ppermute | solution.py:27
  56.4 2.5 %collective-permute-start.17 = (bf16[4,128,256]{2,1,0:T(8,128)(2,1)S(1)}, bf16[4,128,256]{2,1,0:T(8,128)(2,1)S(1)}, u32[]{:S(2)}, u32[]{:S(2)}) collective-permute-start(bf16[4,128,256]{2,1,0:T(8,128)(2,1)S(1)} %get-tuple-element.36), channel_id=1, source_target_pairs={{0,8},{1,9},{2,10},{3,11},{4,12},{5,13},{6,14},{7,15},{8,0},{9,1},... | collective-permute-start | bytes 786440 | tf_op jit(solution)/shard_map/ppermute | solution.py:27
  58.9 4.7 %collective-permute-done.16.refs_1_ = bf16[4,128,256]{2,1,0:T(8,128)(2,1)S(1)} collective-permute-done((bf16[4,128,256]{2,1,0:T(8,128)(2,1)S(1)}, bf16[4,128,256]{2,1,0:T(8,128)(2,1)S(1)}, u32[]{:S(2)}, u32[]{:S(2)}) %collective-permute-start.16) | collective-permute-done | bytes 262176 | tf_op jit(solution)/shard_map/ppermute | solution.py:27
  63.6 12.1 %collective-permute-done.17.refs_2_ = bf16[4,128,256]{2,1,0:T(8,128)(2,1)S(1)} collective-permute-done((bf16[4,128,256]{2,1,0:T(8,128)(2,1)S(1)}, bf16[4,128,256]{2,1,0:T(8,128)(2,1)S(1)}, u32[]{:S(2)}, u32[]{:S(2)}) %collective-permute-start.17) | collective-permute-done | bytes 262176 | tf_op jit(solution)/shard_map/ppermute | solution.py:27
  75.9 5.3 %collective-permute-start.18 = (bf16[128,256]{1,0:T(8,128)(2,1)S(1)}, bf16[128,256]{1,0:T(8,128)(2,1)S(1)}, u32[]{:S(2)}, u32[]{:S(2)}) collective-permute-start(bf16[128,256]{1,0:T(8,128)(2,1)S(1)} %get-tuple-element.38), channel_id=1, source_target_pairs={{0,1},{1,2},{2,3},{3,0},{4,5},{5,6},{6,7},{7,4},{8,9},{9,10},{10,1... | collective-permute-start | bytes 196616 | tf_op jit(solution)/shard_map/ppermute | solution.py:27
  81.2 2.2 %collective-permute-start.20 = (bf16[128,256]{1,0:T(8,128)(2,1)S(1)}, bf16[128,256]{1,0:T(8,128)(2,1)S(1)}, u32[]{:S(2)}, u32[]{:S(2)}) collective-permute-start(bf16[128,256]{1,0:T(8,128)(2,1)S(1)} %get-tuple-element.40), channel_id=1, source_target_pairs={{0,2},{1,3},{2,0},{3,1},{4,6},{5,7},{6,4},{7,5},{8,10},{9,11},{10,... | collective-permute-start | bytes 196616 | tf_op jit(solution)/shard_map/ppermute | solution.py:27
  83.7 3.8 %collective-permute-start.13 = (bf16[128,512]{1,0:T(8,128)(2,1)S(1)}, bf16[128,512]{1,0:T(8,128)(2,1)S(1)}, u32[]{:S(2)}, u32[]{:S(2)}) collective-permute-start(bf16[128,512]{1,0:T(8,128)(2,1)S(1)} %get-tuple-element.31), channel_id=1, source_target_pairs={{0,12},{1,13},{2,14},{3,15},{4,0},{5,1},{6,2},{7,3},{8,4},{9,5},{1... | collective-permute-start | bytes 393224 | tf_op jit(solution)/shard_map/ppermute | solution.py:27
  87.6 4.3 %collective-permute-done.12 = bf16[128,512]{1,0:T(8,128)(2,1)S(1)} collective-permute-done((bf16[128,512]{1,0:T(8,128)(2,1)S(1)}, bf16[128,512]{1,0:T(8,128)(2,1)S(1)}, u32[]{:S(2)}, u32[]{:S(2)}) %collective-permute-start.12) | collective-permute-done | bytes 131104 | tf_op jit(solution)/shard_map/ppermute | solution.py:27
  91.9 5.3 %collective-permute-done.14 = bf16[128,512]{1,0:T(8,128)(2,1)S(1)} collective-permute-done((bf16[128,512]{1,0:T(8,128)(2,1)S(1)}, bf16[128,512]{1,0:T(8,128)(2,1)S(1)}, u32[]{:S(2)}, u32[]{:S(2)}) %collective-permute-start.14) | collective-permute-done | bytes 131104 | tf_op jit(solution)/shard_map/ppermute | solution.py:27
  97.3 0.7 fusion.1
  (54 shorter events, 3.6 us)
Async XLA Ops:
  0.0 12.5 %copy-start.5 = (bf16[128,768]{1,0:T(8,128)(2,1)S(1)}, bf16[128,768]{1,0:T(8,128)(2,1)}, u32[]{:S(2)}) copy-start(bf16[128,768]{1,0:T(8,128)(2,1)} %param.8) | copy-start | bytes 589828
  0.0 17.8 %collective-permute-start.2 = (bf16[128,768]{1,0:T(8,128)(2,1)}, bf16[128,768]{1,0:T(8,128)(2,1)S(1)}, u32[]{:S(2)}, u32[]{:S(2)}) collective-permute-start(bf16[128,768]{1,0:T(8,128)(2,1)} %param.8), channel_id=1, source_target_pairs={{0,96},{16,112},{32,0},{48,16},{64,32},{80,48},{96,64},{112,80},{1... | collective-permute-start | bytes 589832 | tf_op jit(solution)/shard_map/ppermute | solution.py:19
  0.5 17.2 %collective-permute-start.1 = (bf16[128,768]{1,0:T(8,128)(2,1)}, bf16[128,768]{1,0:T(8,128)(2,1)S(1)}, u32[]{:S(2)}, u32[]{:S(2)}) collective-permute-start(bf16[128,768]{1,0:T(8,128)(2,1)} %param.8), channel_id=1, source_target_pairs={{0,32},{16,48},{32,64},{48,80},{64,96},{80,112},{96,0},{112,16},{1... | collective-permute-start | bytes 589832 | tf_op jit(solution)/shard_map/ppermute | solution.py:19
  2.0 11.9 %collective-permute-start = (bf16[128,768]{1,0:T(8,128)(2,1)}, bf16[128,768]{1,0:T(8,128)(2,1)S(1)}, u32[]{:S(2)}, u32[]{:S(2)}) collective-permute-start(bf16[128,768]{1,0:T(8,128)(2,1)} %param.8), channel_id=1, source_target_pairs={{0,128},{16,144},{32,160},{48,176},{64,192},{80,208},{96,224},{112... | collective-permute-start | bytes 589832 | tf_op jit(solution)/shard_map/ppermute | solution.py:19
  9.2 8.7 %collective-permute-start.3 = (bf16[128,768]{1,0:T(8,128)(2,1)}, bf16[128,768]{1,0:T(8,128)(2,1)S(1)}, u32[]{:S(2)}, u32[]{:S(2)}) collective-permute-start(bf16[128,768]{1,0:T(8,128)(2,1)} %param.8), channel_id=1, source_target_pairs={{0,64},{16,80},{32,96},{48,112},{64,0},{80,16},{96,32},{112,48},{1... | collective-permute-start | bytes 589832 | tf_op jit(solution)/shard_map/ppermute | solution.py:19
  13.9 12.7 %collective-permute-start.6 = (bf16[128,768]{1,0:T(8,128)(2,1)S(1)}, bf16[128,768]{1,0:T(8,128)(2,1)S(1)}, u32[]{:S(2)}, u32[]{:S(2)}) collective-permute-start(bf16[128,768]{1,0:T(8,128)(2,1)S(1)} %collective-permute-done), channel_id=1, source_target_pairs={{0,64},{16,80},{32,96},{48,112},{64,0},{80,16},{96,32},{112,48},{1... | collective-permute-start | bytes 589832 | tf_op jit(solution)/shard_map/ppermute | solution.py:19
  15.5 10.4 %collective-permute-start.5 = (bf16[128,768]{1,0:T(8,128)(2,1)S(1)}, bf16[128,768]{1,0:T(8,128)(2,1)S(1)}, u32[]{:S(2)}, u32[]{:S(2)}) collective-permute-start(bf16[128,768]{1,0:T(8,128)(2,1)S(1)} %collective-permute-done), channel_id=1, source_target_pairs={{0,96},{16,112},{32,0},{48,16},{64,32},{80,48},{96,64},{112,80},{1... | collective-permute-start | bytes 589832 | tf_op jit(solution)/shard_map/ppermute | solution.py:19
  17.8 7.4 %collective-permute-start.4 = (bf16[128,768]{1,0:T(8,128)(2,1)S(1)}, bf16[128,768]{1,0:T(8,128)(2,1)S(1)}, u32[]{:S(2)}, u32[]{:S(2)}) collective-permute-start(bf16[128,768]{1,0:T(8,128)(2,1)S(1)} %collective-permute-done), channel_id=1, source_target_pairs={{0,32},{16,48},{32,64},{48,80},{64,96},{80,112},{96,0},{112,16},{1... | collective-permute-start | bytes 589832 | tf_op jit(solution)/shard_map/ppermute | solution.py:19
  17.8 12.1 %copy-start.2 = (bf16[1,1,5,8,128,128]{5,4,3,2,1,0:T(8,128)(2,1)S(1)}, bf16[1,1,5,8,128,128]{5,4,3,2,1,0:T(8,128)(2,1)}, u32[]{:S(2)}) copy-start(bf16[1,1,5,8,128,128]{5,4,3,2,1,0:T(8,128)(2,1)} %param.12) | copy-start | bytes 3932164
  17.9 9.6 %collective-permute-start.7 = (bf16[512,768]{1,0:T(8,128)(2,1)S(1)}, bf16[512,768]{1,0:T(8,128)(2,1)}, u32[]{:S(2)}, u32[]{:S(2)}) collective-permute-start(bf16[512,768]{1,0:T(8,128)(2,1)S(1)} %constant_dynamic-update-slice_fusion.rest_0_), channel_id=1, source_target_pairs={{0,16},{16,0},{32,48},{48,32},{64,80},{80,64},{96,112},{112,96},{1... | collective-permute-start | bytes 2359304 | tf_op jit(solution)/shard_map/ppermute | solution.py:19
  27.2 2.6 %collective-permute-start.8 = (bf16[512,768]{1,0:T(8,128)(2,1)}, bf16[512,768]{1,0:T(8,128)(2,1)}, u32[]{:S(2)}, u32[]{:S(2)}) collective-permute-start(bf16[512,768]{1,0:T(8,128)(2,1)} %constant_dynamic-update-slice_fusion.4.rest_1_), channel_id=1, source_target_pairs={{0,16},{16,0},{32,48},{48,32},{64,80},{80,64},{96,112},{112,96},{1... | collective-permute-start | bytes 2359304 | tf_op jit(solution)/shard_map/ppermute | solution.py:19
  43.9 12.5 %collective-permute-start.15 = (bf16[4,128,256]{2,1,0:T(8,128)(2,1)S(1)}, bf16[4,128,256]{2,1,0:T(8,128)(2,1)S(1)}, u32[]{:S(2)}, u32[]{:S(2)}) collective-permute-start(bf16[4,128,256]{2,1,0:T(8,128)(2,1)S(1)} %get-tuple-element.34), channel_id=1, source_target_pairs={{0,4},{1,5},{2,6},{3,7},{4,8},{5,9},{6,10},{7,11},{8,12},{9,13},{1... | collective-permute-start | bytes 786440 | tf_op jit(solution)/shard_map/ppermute | solution.py:27
  51.9 29.2 %collective-permute-start.9 = (bf16[4,128,512]{2,1,0:T(8,128)(2,1)S(1)}, bf16[4,128,512]{2,1,0:T(8,128)(2,1)S(1)}, u32[]{:S(2)}, u32[]{:S(2)}) collective-permute-start(bf16[4,128,512]{2,1,0:T(8,128)(2,1)S(1)} %get-tuple-element.26), channel_id=1, source_target_pairs={{0,1},{1,2},{2,3},{3,0},{4,5},{5,6},{6,7},{7,4},{8,9},{9,10},{10,1... | collective-permute-start | bytes 1572872 | tf_op jit(solution)/shard_map/ppermute | solution.py:27
  51.9 31.4 %collective-permute-start.10 = (bf16[4,128,512]{2,1,0:T(8,128)(2,1)S(1)}, bf16[4,128,512]{2,1,0:T(8,128)(2,1)S(1)}, u32[]{:S(2)}, u32[]{:S(2)}) collective-permute-start(bf16[4,128,512]{2,1,0:T(8,128)(2,1)S(1)} %get-tuple-element.27), channel_id=1, source_target_pairs={{0,3},{1,0},{2,1},{3,2},{4,7},{5,4},{6,5},{7,6},{8,11},{9,8},{10,9... | collective-permute-start | bytes 1572872 | tf_op jit(solution)/shard_map/ppermute | solution.py:27
  55.2 28.2 %collective-permute-start.11 = (bf16[4,128,512]{2,1,0:T(8,128)(2,1)S(1)}, bf16[4,128,512]{2,1,0:T(8,128)(2,1)S(1)}, u32[]{:S(2)}, u32[]{:S(2)}) collective-permute-start(bf16[4,128,512]{2,1,0:T(8,128)(2,1)S(1)} %get-tuple-element.28), channel_id=1, source_target_pairs={{0,2},{1,3},{2,0},{3,1},{4,6},{5,7},{6,4},{7,5},{8,10},{9,11},{10,... | collective-permute-start | bytes 1572872 | tf_op jit(solution)/shard_map/ppermute | solution.py:27
  55.2 8.4 %collective-permute-start.16 = (bf16[4,128,256]{2,1,0:T(8,128)(2,1)S(1)}, bf16[4,128,256]{2,1,0:T(8,128)(2,1)S(1)}, u32[]{:S(2)}, u32[]{:S(2)}) collective-permute-start(bf16[4,128,256]{2,1,0:T(8,128)(2,1)S(1)} %get-tuple-element.35), channel_id=1, source_target_pairs={{0,12},{1,13},{2,14},{3,15},{4,0},{5,1},{6,2},{7,3},{8,4},{9,5},{1... | collective-permute-start | bytes 786440 | tf_op jit(solution)/shard_map/ppermute | solution.py:27
  56.4 19.3 %collective-permute-start.17 = (bf16[4,128,256]{2,1,0:T(8,128)(2,1)S(1)}, bf16[4,128,256]{2,1,0:T(8,128)(2,1)S(1)}, u32[]{:S(2)}, u32[]{:S(2)}) collective-permute-start(bf16[4,128,256]{2,1,0:T(8,128)(2,1)S(1)} %get-tuple-element.36), channel_id=1, source_target_pairs={{0,8},{1,9},{2,10},{3,11},{4,12},{5,13},{6,14},{7,15},{8,0},{9,1},... | collective-permute-start | bytes 786440 | tf_op jit(solution)/shard_map/ppermute | solution.py:27
  75.9 11.6 %collective-permute-start.18 = (bf16[128,256]{1,0:T(8,128)(2,1)S(1)}, bf16[128,256]{1,0:T(8,128)(2,1)S(1)}, u32[]{:S(2)}, u32[]{:S(2)}) collective-permute-start(bf16[128,256]{1,0:T(8,128)(2,1)S(1)} %get-tuple-element.38), channel_id=1, source_target_pairs={{0,1},{1,2},{2,3},{3,0},{4,5},{5,6},{6,7},{7,4},{8,9},{9,10},{10,1... | collective-permute-start | bytes 196616 | tf_op jit(solution)/shard_map/ppermute | solution.py:27
  81.2 6.3 %collective-permute-start.19 = (bf16[128,256]{1,0:T(8,128)(2,1)S(1)}, bf16[128,256]{1,0:T(8,128)(2,1)S(1)}, u32[]{:S(2)}, u32[]{:S(2)}) collective-permute-start(bf16[128,256]{1,0:T(8,128)(2,1)S(1)} %get-tuple-element.39), channel_id=1, source_target_pairs={{0,3},{1,0},{2,1},{3,2},{4,7},{5,4},{6,5},{7,6},{8,11},{9,8},{10,9... | collective-permute-start | bytes 196616 | tf_op jit(solution)/shard_map/ppermute | solution.py:27
  81.2 6.3 %collective-permute-start.20 = (bf16[128,256]{1,0:T(8,128)(2,1)S(1)}, bf16[128,256]{1,0:T(8,128)(2,1)S(1)}, u32[]{:S(2)}, u32[]{:S(2)}) collective-permute-start(bf16[128,256]{1,0:T(8,128)(2,1)S(1)} %get-tuple-element.40), channel_id=1, source_target_pairs={{0,2},{1,3},{2,0},{3,1},{4,6},{5,7},{6,4},{7,5},{8,10},{9,11},{10,... | collective-permute-start | bytes 196616 | tf_op jit(solution)/shard_map/ppermute | solution.py:27
  83.6 13.7 %copy-start.4 = (f32[128,768]{1,0:T(8,128)S(1)}, f32[128,768]{1,0:T(8,128)}, u32[]{:S(2)}) copy-start(f32[128,768]{1,0:T(8,128)} %convolution_add_fusion) | copy-start | bytes 1179652
  83.6 8.3 %collective-permute-start.12 = (bf16[128,512]{1,0:T(8,128)(2,1)S(1)}, bf16[128,512]{1,0:T(8,128)(2,1)S(1)}, u32[]{:S(2)}, u32[]{:S(2)}) collective-permute-start(bf16[128,512]{1,0:T(8,128)(2,1)S(1)} %get-tuple-element.30), channel_id=1, source_target_pairs={{0,4},{1,5},{2,6},{3,7},{4,8},{5,9},{6,10},{7,11},{8,12},{9,13},{1... | collective-permute-start | bytes 393224 | tf_op jit(solution)/shard_map/ppermute | solution.py:27
  83.7 8.2 %collective-permute-start.13 = (bf16[128,512]{1,0:T(8,128)(2,1)S(1)}, bf16[128,512]{1,0:T(8,128)(2,1)S(1)}, u32[]{:S(2)}, u32[]{:S(2)}) collective-permute-start(bf16[128,512]{1,0:T(8,128)(2,1)S(1)} %get-tuple-element.31), channel_id=1, source_target_pairs={{0,12},{1,13},{2,14},{3,15},{4,0},{5,1},{6,2},{7,3},{8,4},{9,5},{1... | collective-permute-start | bytes 393224 | tf_op jit(solution)/shard_map/ppermute | solution.py:27
  87.5 9.7 %collective-permute-start.14 = (bf16[128,512]{1,0:T(8,128)(2,1)S(1)}, bf16[128,512]{1,0:T(8,128)(2,1)S(1)}, u32[]{:S(2)}, u32[]{:S(2)}) collective-permute-start(bf16[128,512]{1,0:T(8,128)(2,1)S(1)} %get-tuple-element.32), channel_id=1, source_target_pairs={{0,8},{1,9},{2,10},{3,11},{4,12},{5,13},{6,14},{7,15},{8,0},{9,1},... | collective-permute-start | bytes 393224 | tf_op jit(solution)/shard_map/ppermute | solution.py:27
  (5 other events, 44.2 us)
